TPU v7x, 32 devices: a whole 2x2x4 slice. The times are simulated.
32 devices in a mesh: seq: 16 (over z, x, core), head: 2 (over y).
Axes of the slice: x: 2, y: 2, z: 4, core: 2. Of those that a mesh axis runs over, the one named last changes fastest.
Arguments:
- query_rows: bfloat16 [16384, 128], P('seq'), may hold values from -6 to 6
- key_rows: bfloat16 [16384, 128], P('seq'), may hold values from -6 to 6
- value_rows: bfloat16 [16384, 4096], P('seq', 'head'), may hold values from -6 to 6
- gate_rows: bfloat16 [16384, 4096], P('seq', 'head'), may hold values from -6 to 6
- norm_gain: float32 [4096], P('head'), may hold values from 0.25 to 1.75
- level_table: float32 [16], replicated, may hold values from 0.25 to 4
- level_index: int32 [32, 11], P('head'), may hold values from 0 to 15
- out_weight: bfloat16 [2048, 4096], P('seq', 'head'), may hold values from -0.09375 to 0.09375
Outputs:
- mixed_tokens: bfloat16 [16384, 2048], P('seq', 'head')
All inputs are finite; a program needn't handle non-finite values.
Results may differ from a plain program's by a relative error of at most 0.014.
Values may be sent and summed in bfloat16 or wider, within the bound.
A program may use at most 128 MiB of HBM per device.

v0:
```python
import jax
import jax.numpy as jnp
from jax import lax
from jax.sharding import PartitionSpec as P

BLOCK = 64
INNER = 4096


EPSILON = 1e-05


def partner_2(block, axis, stride):
    count = lax.axis_size(axis)
    route = []
    for low in range(count):
        high = low | 1 << stride
        if high != low and high < count:
            route += [(low, high), (high, low)]
    return lax.ppermute(block, axis, route)


def body(
    query_rows, key_rows, value_rows, gate_rows, norm_gain, level_table, level_index, out_weight
):
    tok_rows = query_rows.shape[0]
    blocks = tok_rows // BLOCK
    col_width = value_rows.shape[1]
    heads_here = level_index.shape[0]
    head_width = col_width // heads_here
    levels_here = blocks.bit_length() - 1
    seq_bits = lax.axis_size("seq").bit_length() - 1
    choose = (level_index[:, :, None] == jnp.arange(level_table.shape[0], dtype=jnp.int32)).astype(
        jnp.float32
    )
    picked = jnp.sum(choose * level_table, axis=2)
    tiers = jnp.arange(level_index.shape[1])
    bucket_sizes = BLOCK * jnp.exp2(jnp.maximum(tiers - 1, 0).astype(jnp.float32))
    weights = picked / jnp.sqrt(bucket_sizes)
    column_weights = jnp.repeat(weights, head_width, axis=0).T
    query_blocks = query_rows.reshape(blocks, BLOCK, query_rows.shape[1])
    key_blocks = key_rows.reshape(blocks, BLOCK, key_rows.shape[1])
    value_blocks = value_rows.reshape(blocks, BLOCK, col_width)
    positions = jnp.arange(BLOCK)
    causal_mask = (positions[:, None] >= positions[None, :]).astype(jnp.float32)
    scores = jnp.einsum(
        "ctn,csn->cts", query_blocks, key_blocks, preferred_element_type=jnp.float32
    )
    masked = (scores * causal_mask).astype(jnp.bfloat16)
    inside = jnp.einsum("cts,csp->ctp", masked, value_blocks, preferred_element_type=jnp.float32)
    states = jnp.einsum(
        "csn,csp->cnp", key_blocks, value_blocks, preferred_element_type=jnp.float32
    )
    combined = jnp.zeros_like(states)
    for tier_num in range(1, levels_here + 1):
        span_width = 2 ** (tier_num - 1)
        groups = blocks // (2 * span_width)
        shaped = states.reshape(groups, 2, span_width, states.shape[1], col_width)
        lower_sum = jnp.sum(shaped[:, 0], axis=1)
        placed = jnp.stack(
            [jnp.zeros_like(lower_sum), lower_sum * column_weights[tier_num]], axis=1
        )
        combined = combined + jnp.broadcast_to(placed[:, :, None], shaped.shape).reshape(
            states.shape
        )
    own_total = jnp.sum(states, axis=0)
    across = jnp.zeros_like(own_total)
    position = lax.axis_index("seq")
    for bit_num in range(seq_bits):
        partner = partner_2(own_total, "seq", bit_num)
        has_bit = position >> bit_num & 1 == 1
        across = across + jnp.where(
            has_bit, partner * column_weights[levels_here + 1 + bit_num], 0.0
        )
        own_total = own_total + partner
    carried = (combined + across[None]).astype(jnp.bfloat16)
    past_part = jnp.einsum(
        "ctn,cnp->ctp", query_blocks, carried, preferred_element_type=jnp.float32
    )
    mixed_rows = (column_weights[0] * inside + past_part).reshape(tok_rows, col_width)
    gated_rows = mixed_rows * jax.nn.silu(gate_rows.astype(jnp.float32))
    square_sum = lax.psum(jnp.sum(gated_rows * gated_rows, axis=1), "head")
    normed = (gated_rows * lax.rsqrt(square_sum[:, None] / INNER + EPSILON) * norm_gain).astype(
        jnp.bfloat16
    )
    partial_rows = lax.dot_general(
        normed,
        lax.all_gather(out_weight, "seq", axis=0, tiled=True),
        (((1,), (1,)), ((), ())),
        preferred_element_type=jnp.float32,
    )
    mixed_out = lax.psum_scatter(
        partial_rows.astype(jnp.bfloat16), "head", scatter_dimension=1, tiled=True
    )
    return mixed_out


def solution(mesh):
    in_specs = (
        P("seq", None),
        P("seq", None),
        P("seq", "head"),
        P("seq", "head"),
        P("head"),
        P(),
        P("head", None),
        P("seq", "head"),
    )
    out_specs = P("seq", "head")
    return jax.shard_map(body, mesh=mesh, in_specs=in_specs, out_specs=out_specs, check_vma=False)
```

profile of v0, /device:TPU:0, one launch (start us, length us, event | category | flops | bytes accessed | tf_op | source)
XLA Modules:
  0.0 258.1 jit_solution(4367316270785118177)
XLA Ops:
  6.5 0.0 copy-start
  6.5 0.7 all-gather.2.cloned.1.call-update
  7.3 0.0 reduce-scatter.2.cloned.1.call-start
  7.3 0.2 copy-done
  7.5 10.4 %fusion.18 = (f32[128,2048]{1,0:T(8,128)S(1)}, f32[16,128,2048]{2,1,0:T(8,128)}) fusion(bf16[16,64,128]{2,1,0:T(8,128)(2,1)S(1)} %bitcast.70, bf16[16,64,2048]{2,1,0:T(8,128)(2,1)} %bitcast.75), kind=kOutput, calls=%fused_computation.42 | convolution fusion | flops 540803072 | bytes 22282240 | tf_op jit(solution)/shard_map/csn,csp->cnp/dot_general | solution.py:51
  17.9 0.5 collective-permute-start
  18.4 0.1 copy.11
  18.5 0.2 select_reduce_fusion
  18.6 0.1 broadcast_divide_fusion
  18.7 5.0 %slice_reduce_fusion.1 = f32[2,128,2048]{2,1,0:T(8,128)S(1)} fusion(f32[2,2,4,128,2048]{4,3,2,1,0:T(8,128)} %bitcast.71), kind=kLoop, calls=%fused_computation.12 | loop fusion | flops 1572864 | bytes 10485760 | tf_op jit(solution)/shard_map/reduce_sum | solution.py:59
  23.7 0.1 broadcast_bitcast_fusion
  23.9 0.1 fusion.17
  23.9 1.6 bitcast_multiply_fusion.1
  25.5 0.0 collective-permute-done
  25.5 1.2 add.69
  26.7 2.3 collective-permute-start.1
  29.1 1.1 slice_reduce_fusion.2
  30.2 2.5 bitcast_multiply_fusion
  32.6 26.8 %collective-permute-done.1 = f32[128,2048]{1,0:T(8,128)} collective-permute-done((f32[128,2048]{1,0:T(8,128)}, f32[128,2048]{1,0:T(8,128)}, u32[]{:S(2)}, u32[]{:S(2)}) %collective-permute-start.1) | collective-permute-done | bytes 1048608 | tf_op jit(solution)/shard_map/ppermute | solution.py:20
  59.4 1.7 add.71
  61.1 1.6 collective-permute-start.2
  62.7 0.8 slice_reduce_fusion
  63.5 4.1 %fusion.7 = f32[8,1,128,2048]{3,2,1,0:T(8,128)} fusion(f32[8,2,1,128,2048]{4,3,1,0,2:T(8,128)S(1)} %bitcast.74, f32[2048]{0:T(1024)S(1)} %bitcast.89), kind=kLoop, calls=%fused_computation.16 | loop fusion | flops 2097152 | bytes 16785408
  67.6 36.5 %collective-permute-done.2 = f32[128,2048]{1,0:T(8,128)S(1)} collective-permute-done((f32[128,2048]{1,0:T(8,128)S(1)}, f32[128,2048]{1,0:T(8,128)S(1)}, u32[]{:S(2)}, u32[]{:S(2)}) %collective-permute-start.2) | collective-permute-done | bytes 1048608 | tf_op jit(solution)/shard_map/ppermute | solution.py:20
  104.1 1.0 copy-done.5
  105.1 1.1 add.73
  106.2 2.5 collective-permute-start.3
  108.6 1.1 bitcast_multiply_fusion.2
  109.7 11.5 %stack.16.clone = f32[8,2,128,2048]{3,2,1,0:T(8,128)} pad(f32[8,1,128,2048]{3,2,1,0:T(8,128)} %fusion.7, f32[]{:T(128)} %constant.13.clone.1), padding=0_0x1_0x0_0x0_0 | pad | bytes 25165828 | tf_op jit(solution)/shard_map/stack | solution.py:60
  121.2 0.0 copy-done.3
  121.2 4.2 %stack.17 = f32[4,2,128,2048]{3,2,1,0:T(8,128)} pad(f32[4,1,128,2048]{3,2,1,0:T(8,128)S(1)} %copy-done.3, f32[]{:T(128)} %constant.13.clone.1), padding=0_0x1_0x0_0x0_0 | pad | bytes 12582916 | tf_op jit(solution)/shard_map/stack | solution.py:60
  125.4 2.5 stack.18
  127.9 0.2 pad_bitcast_fusion
  128.1 6.9 %fusion.13 = f32[16,64,2048]{2,1,0:T(8,128)} fusion(bf16[16,64,2048]{2,1,0:T(8,128)(2,1)} %bitcast.76, bf16[16,64,128]{2,1,0:T(8,128)(2,1)} %bitcast.79, bf16[16,64,128]{2,1,0:T(8,128)(2,1)S(1)} %bitcast.69, f32[64,64]{1,0:T(8,128)S(1)} %fusion.15), kind=kOutput, calls=%fused_computation.29 | convolution fusion | flops 285343744 | bytes 13123584 | tf_op jit(solution)/shard_map/cts,csp->ctp/dot_general | solution.py:50
  135.0 19.1 %collective-permute-done.3 = f32[128,2048]{1,0:T(8,128)} collective-permute-done((f32[128,2048]{1,0:T(8,128)}, f32[128,2048]{1,0:T(8,128)}, u32[]{:S(2)}, u32[]{:S(2)}) %collective-permute-start.3) | collective-permute-done | bytes 1048608 | tf_op jit(solution)/shard_map/ppermute | solution.py:20
  154.1 2.4 select_add_fusion
  156.6 0.0 slice-start.1
  156.6 0.0 copy-start.7
  156.6 11.8 %fusion.1 = bf16[16,128,2048]{2,1,0:T(8,128)(2,1)S(1)} fusion(f32[8,2,128,2048]{3,2,1,0:T(8,128)} %stack.16.clone, f32[128,2048]{1,0:T(8,128)S(1)} %select_add_fusion, f32[2,128,2048]{2,1,0:T(8,128)S(1)} %pad_bitcast_fusion, f32[2,2,128,2048]{3,2,1,0:T(8,128)} %stack.18, f32[4,2,128,2048]{3,2,1,0:T(8,128)} %stack.17), kind=kLoop, calls=%fused_computation.2 | loop fusion | flops 20971520 | bytes 40894464 | tf_op jit(solution)/shard_map/convert_element_type | solution.py:76
  168.5 1.4 bitcast_add_fusion.3
  169.9 0.0 copy-start.10
  169.9 7.7 %multiply_reduce_fusion = (f32[1024]{0:T(1024)S(1)}, f32[1024,2048]{1,0:T(8,128)}) fusion(bf16[1024,2048]{1,0:T(8,128)(2,1)} %param.11, f32[16,64,2048]{2,1,0:T(8,128)S(1)} %bitcast_add_fusion.3), kind=kLoop, calls=%fused_computation.19 | loop fusion | flops 16776192 | bytes 20975616 | tf_op jit(solution)/shard_map/reduce_sum | solution.py:82
  177.6 4.9 %psum.7 = f32[1024]{0:T(1024)S(1)} all-reduce(f32[1024]{0:T(1024)S(1)} %get-tuple-element.5), channel_id=1, replica_groups=mesh['seq'=16,'head'=2] {'head'}, use_global_device_ids=true, to_apply=%region_6.7 | all-reduce | flops 1024 | bytes 8192 | tf_op jit(solution)/shard_map/psum | solution.py:82
  182.5 0.0 all-gather.2.cloned.1.call-done
  182.5 0.0 copy-start.1
  182.5 15.3 %fusion.11 = bf16[1024,2048]{1,0:T(8,128)(2,1)} fusion(bf16[2048,2048]{1,0:T(8,128)(2,1)} %all-gather.2.cloned.1.call-done, f32[1024,2048]{1,0:T(8,128)} %get-tuple-element.6, f32[2048]{0:T(1024)S(1)} %copy-done.10, f32[1024]{0:T(1024)S(1)} %add_rsqrt_fusion), kind=kOutput, calls=%fused_computation.24 | convolution fusion | flops 8598323200 | bytes 20983808 | tf_op jit(solution)/shard_map/dot_general | solution.py:86
  197.8 0.0 reduce-scatter.2.cloned.1.call-update
  197.8 53.4 %reduce-scatter.2.cloned.1.call-done = bf16[1024,1024]{1,0:T(8,128)(2,1)} async-done(((bf16[1024,2048]{1,0:T(8,128)(2,1)}), bf16[1024,1024]{1,0:T(8,128)(2,1)}) %reduce-scatter.2.cloned.1.call-update) | async-done | bytes 2097168 | tf_op jit(solution)/shard_map/reduce_scatter | solution.py:92
  (25 shorter events, 0.1 us)
Async XLA Ops:
  6.5 1.0 copy-start
  6.5 175.9 %all-gather.2.cloned.1.call-start = ((), (), s32[]{:S(2)}) async-start(), calls=%async_computation.1 | async-start | bytes 8912896 | tf_op jit(solution)/shard_map/all_gather | solution.py:88
  7.3 244.0 %reduce-scatter.2.cloned.1.call-start = ((), (), s32[]{:S(2)}) async-start(), calls=%async_computation.2 | async-start | bytes 6291456 | tf_op jit(solution)/shard_map/reduce_scatter | solution.py:92
  7.5 10.9 %copy-start.8 = (s32[16,11]{1,0:T(8,128)S(1)}, s32[16,11]{1,0:T(8,128)}, u32[]{:S(2)}) copy-start(s32[16,11]{1,0:T(8,128)} %param.14) | copy-start | bytes 2116
  7.5 11.0 %copy-start.9 = (f32[16]{0:T(128)S(1)}, f32[16]{0:T(128)}, u32[]{:S(2)}) copy-start(f32[16]{0:T(128)} %param.13) | copy-start | bytes 196
  17.9 7.7 %collective-permute-start = (f32[128,2048]{1,0:T(8,128)S(1)}, f32[128,2048]{1,0:T(8,128)S(1)}, u32[]{:S(2)}, u32[]{:S(2)}) collective-permute-start(f32[128,2048]{1,0:T(8,128)S(1)} %get-tuple-element.16), channel_id=1, source_target_pairs={{0,2},{2,0},{4,6},{6,4},{8,10},{10,8},{12,14},{14,12},{16,18},{18,... | collective-permute-start | bytes 3145736 | tf_op jit(solution)/shard_map/ppermute | solution.py:20
  18.7 10.3 %copy-start.2 = (f32[16,128,2048]{2,1,0:T(8,128)S(1)}, f32[16,128,2048]{2,1,0:T(8,128)}, u32[]{:S(2)}) copy-start(f32[16,128,2048]{2,1,0:T(8,128)} %get-tuple-element.17) | copy-start | bytes 50331652
  26.7 32.7 %collective-permute-start.1 = (f32[128,2048]{1,0:T(8,128)}, f32[128,2048]{1,0:T(8,128)}, u32[]{:S(2)}, u32[]{:S(2)}) collective-permute-start(f32[128,2048]{1,0:T(8,128)} %add.69), channel_id=1, source_target_pairs={{0,4},{4,0},{2,6},{6,2},{8,12},{12,8},{10,14},{14,10},{16,20},{20,... | collective-permute-start | bytes 3145736 | tf_op jit(solution)/shard_map/ppermute | solution.py:20
  61.1 43.0 %collective-permute-start.2 = (f32[128,2048]{1,0:T(8,128)S(1)}, f32[128,2048]{1,0:T(8,128)S(1)}, u32[]{:S(2)}, u32[]{:S(2)}) collective-permute-start(f32[128,2048]{1,0:T(8,128)S(1)} %add.71), channel_id=1, source_target_pairs={{0,8},{8,0},{2,10},{10,2},{4,12},{12,4},{6,14},{14,6},{16,24},{24,... | collective-permute-start | bytes 3145736 | tf_op jit(solution)/shard_map/ppermute | solution.py:20
  104.1 1.0 copy-start.5
  106.2 47.9 %collective-permute-start.3 = (f32[128,2048]{1,0:T(8,128)}, f32[128,2048]{1,0:T(8,128)}, u32[]{:S(2)}, u32[]{:S(2)}) collective-permute-start(f32[128,2048]{1,0:T(8,128)} %add.73), channel_id=1, source_target_pairs={{0,16},{16,0},{2,18},{18,2},{4,20},{20,4},{6,22},{22,6},{8,24},{24... | collective-permute-start | bytes 3145736 | tf_op jit(solution)/shard_map/ppermute | solution.py:20
  109.7 11.5 %copy-start.3 = (f32[4,1,128,2048]{3,2,1,0:T(8,128)S(1)}, f32[4,1,128,2048]{3,2,1,0:T(8,128)}, u32[]{:S(2)}) copy-start(f32[4,1,128,2048]{3,2,1,0:T(8,128)} %bitcast_multiply_fusion) | copy-start | bytes 12582916
  121.2 4.2 %copy-start.4 = (f32[2,1,128,2048]{3,2,1,0:T(8,128)S(1)}, f32[2,1,128,2048]{3,2,1,0:T(8,128)}, u32[]{:S(2)}) copy-start(f32[2,1,128,2048]{3,2,1,0:T(8,128)} %bitcast_multiply_fusion.1) | copy-start | bytes 6291460
  121.2 6.8 %copy-start.6 = (f32[1,1,128,2048]{3,2,1,0:T(8,128)S(1)}, f32[1,1,128,2048]{3,2,1,0:T(8,128)}, u32[]{:S(2)}) copy-start(f32[1,1,128,2048]{3,2,1,0:T(8,128)} %bitcast_multiply_fusion.2) | copy-start | bytes 3145732
  154.1 14.3 %slice-start = ((s8[8388608]{0:T(1024)(128)(4,1)}), s8[4194304]{0:T(1024)(128)(4,1)S(1)}, s32[]{:S(2)}) async-start(s8[8388608]{0:T(1024)(128)(4,1)} %bitcast.77), calls=%async_computation.3 | async-start | bytes 8388608
  156.6 11.9 %slice-start.1 = ((s8[8388608]{0:T(1024)(128)(4,1)}), s8[4194304]{0:T(1024)(128)(4,1)S(1)}, s32[]{:S(2)}) async-start(s8[8388608]{0:T(1024)(128)(4,1)} %bitcast.77), calls=%async_computation.4 | async-start | bytes 8388608
  156.6 11.9 %copy-start.7 = (bf16[1024,128]{1,0:T(8,128)(2,1)S(1)}, bf16[1024,128]{1,0:T(8,128)(2,1)}, u32[]{:S(2)}) copy-start(bf16[1024,128]{1,0:T(8,128)(2,1)} %param.8) | copy-start | bytes 786436
  169.9 12.6 %copy-start.10 = (f32[2048]{0:T(1024)S(1)}, f32[2048]{0:T(1024)}, u32[]{:S(2)}) copy-start(f32[2048]{0:T(1024)} %param.12) | copy-start | bytes 24580
  182.5 68.7 %copy-start.1 = (bf16[1024,128]{1,0:T(8,128)(2,1)S(1)}, bf16[1024,128]{1,0:T(8,128)(2,1)}, u32[]{:S(2)}) copy-start(bf16[1024,128]{1,0:T(8,128)(2,1)} %param.9) | copy-start | bytes 786436
Sparse Core Ops, SparseCore 0:
  9.5 89.7 all-gather.1
  197.9 53.2 reduce-scatter.1
where the time goes:
time: 258 us
  waiting for transfers between devices  137 us (53%)
  other arithmetic  42.3 us (16%)
  matrix products  33.9 us (13%)
  local copies, waits for them, and re-layouts  19.9 us (8%)
  between operations  13.6 us (5%)
  starting transfers between devices  6.89 us (3%)
  blocking collectives  4.91 us (2%)
    ppermute x4, waiting for transfers between devices, partner_2(): return lax.ppermute(block, axis, route)  82.4 us
    reduce_scatter x1, waiting for transfers between devices, body(): lax.psum_scatter(partial_rows.astype(jnp.bfloat16), 'head', scatter_dimen...  53.4 us
    another operation x3, local copies, waits for them, and re-layouts, body(): jnp.stack([jnp.zeros_like(lower_sum), lower_sum * column_weights[tier_num...  18.2 us
    dot_general x1, matrix products, body(): lax.dot_general(normed, lax.all_gather(out_weight, 'seq', axis=0, tiled=T...  15.3 us
    convert_element_type x1, other arithmetic, body(): carried = (combined + across[None]).astype(jnp.bfloat16)  11.8 us
    dot_general x1, matrix products, body(): jnp.einsum('csn,csp->cnp', key_blocks, value_blocks, preferred_element_ty...  10.4 us
    reduce_sum x1, other arithmetic, body(): square_sum = lax.psum(jnp.sum(gated_rows * gated_rows, axis=1), 'head')  7.67 us
    reduce_sum x3, other arithmetic, body(): lower_sum = jnp.sum(shaped[:, 0], axis=1)  6.87 us
  transfers between devices with their start and end apart: 6, of which 4 were waited for; matrix products, arithmetic and copies ran while one was open for 31% of the time, Pallas kernels for 0%

commit v1 on v0

v1 whole, which is shorter than its diff:
```python
import functools

import jax
import jax.numpy as jnp
from jax import lax
from jax.experimental import pallas as pl
from jax.experimental.pallas import tpu as pltpu
from jax.sharding import PartitionSpec as P

BLOCK = 64
INNER = 4096
EPSILON = 1e-05
F32 = jnp.float32
BF16 = jnp.bfloat16
MESH = pl.DeviceIdType.MESH


def dot(a, b, dims):
    return lax.dot_general(a, b, (dims, ((), ())), preferred_element_type=F32)


def kernel(
    S, H, q_ref, k_ref, v_ref, gate_hbm, gain_ref, lam_ref, w_hbm, out_ref,
    gate, wbuf, loc, gbuf, gsc, tot, tb, rsib, half_f, half_b, r1, qf, qb, rq, xs, xr, hs, hr, acr,
    ssq_own, ssq_all, psend, precv, pown,
    lsem, ssem, rsem, wr, wa, wb, wc, qs, qr, ps, pr,
):
    tok, state = q_ref.shape
    cols = v_ref.shape[1]
    mr = w_hbm.shape[0]
    blocks = tok // BLOCK
    levels = blocks.bit_length() - 1
    nbits = S.bit_length() - 1
    qw = cols // 4
    A = min(4, S // 2)
    B = S // (2 * A)
    s = lax.axis_index("seq")
    h = lax.axis_index("head")
    core, b_pos, a_pos = s % 2, (s // 2) % B, s // (2 * B)

    barrier = pltpu.get_barrier_semaphore()
    for d in range(1, S):
        pl.semaphore_signal(barrier, inc=1, device_id={"seq": (s + d) % S}, device_id_type=MESH)
    for d in range(1, H):
        pl.semaphore_signal(barrier, inc=1, device_id={"head": (h + d) % H}, device_id_type=MESH)
    gate_copy = pltpu.make_async_copy(gate_hbm, gate, lsem.at[0])
    gate_copy.start()
    own_copy = pltpu.make_async_copy(w_hbm, wbuf.at[s], lsem.at[1])
    own_copy.start()

    for i in range(4):
        t = dot(k_ref[...], v_ref[:, i * qw:(i + 1) * qw], ((0,), (0,)))
        tot[i] = t
        tb[i] = t.astype(BF16)
    pl.semaphore_wait(barrier, S + H - 2)

    pending = []

    def remote(src, dst, send, recv, target):
        return pltpu.make_async_remote_copy(
            src_ref=src, dst_ref=dst, send_sem=send, recv_sem=recv,
            device_id=target, device_id_type=MESH,
        )

    def when(cond, fn):
        if cond is True:
            fn()
        else:
            pl.when(cond)(fn)

    def w_send(cond, block, own, target, sem):
        copy = remote(w_hbm if own else wbuf.at[block], wbuf.at[block], sem, wr.at[block], {"seq": target})
        when(cond, lambda: copy.start())
        pending.append((cond, copy))

    def w_wait(cond, block, sem):
        copy = remote(wbuf.at[block], wbuf.at[block], sem, wr.at[block], {"seq": s ^ 1})
        when(cond, lambda: copy.wait_recv())

    def both(x, y):
        return y if x is True else (x if y is True else jnp.logical_and(x, y))

    def blk(a, b, c):
        return (a * B + b) * 2 + c

    def clamp(x, n):
        return jnp.minimum(jnp.maximum(x, 0), n - 1)

    def send_b(cond, ab, own):
        block = blk(ab, b_pos, core)
        if B > 1:
            w_send(both(cond, b_pos < B - 1), block, own, blk(a_pos, clamp(b_pos + 1, B), core), wb.at[0, ab * B + b_pos])
            w_send(both(cond, b_pos > 0), block, own, blk(a_pos, clamp(b_pos - 1, B), core), wb.at[1, ab * B + b_pos])

    def send_core(cond, ab, bb, own):
        w_send(cond, blk(ab, bb, core), own, s ^ 1, wc.at[ab * B + bb])

    def step_a(j):
        for sign in (1, -1):
            ab = a_pos - sign * j
            cond = ab >= 0 if sign == 1 else ab <= A - 1
            ab = clamp(ab, A)
            block = blk(ab, b_pos, core)
            w_wait(cond, block, wc.at[0])
            onward = a_pos < A - 1 if sign == 1 else a_pos > 0
            nxt = clamp(a_pos + sign, A)
            w_send(both(cond, onward), block, False, blk(nxt, b_pos, core), wa.at[(1 - sign) // 2, ab])
            send_b(cond, ab, False)
            send_core(cond, ab, b_pos, False)

    def steps_b():
        for j in range(1, B):
            for sign in (1, -1):
                bb = b_pos - sign * j
                cond = bb >= 0 if sign == 1 else bb <= B - 1
                bb = clamp(bb, B)
                onward = both(cond, b_pos < B - 1 if sign == 1 else b_pos > 0)
                for i in range(A):
                    ab = lax.rem(a_pos + i, A)
                    block = blk(ab, bb, core)
                    w_wait(cond, block, wc.at[0])
                    if B > 2:
                        w_send(onward, block, False, blk(a_pos, clamp(b_pos + sign, B), core), wb.at[(1 - sign) // 2, ab * B + bb])
                    send_core(cond, ab, bb, False)

    def s_send(i, src, dst, target):
        copy = remote(src, dst, ssem.at[i], rsem.at[i], {"seq": target})
        copy.start()
        return copy

    tw = min(256, cols)
    tiles = cols // tw

    def local_tiles(lo, hi):
        @pl.loop(lo, hi)
        def _(ct):
            at = pl.ds(pl.multiple_of(ct * tw, tw), tw)
            lam = lam_ref[:, at]

            def vals(c):
                return v_ref[pl.ds(c * BLOCK, BLOCK), at]

            def total(lo_c, n):
                if n == 1:
                    r = pl.ds(lo_c * BLOCK, BLOCK)
                    return dot(k_ref[r, :], vals(lo_c), ((0,), (0,)))
                return sums[(lo_c, n // 2)] + sums[(lo_c + n // 2, n // 2)]

            sums = {}
            n = 1
            while n < blocks:
                for lo_c in range(0, blocks, n):
                    sums[(lo_c, n)] = total(lo_c, n)
                n *= 2

            def walk(lo_c, n, base):
                if n == 1:
                    r = pl.ds(lo_c * BLOCK, BLOCK)
                    m = lam[0:1] * dot(gsc[lo_c], vals(lo_c), ((1,), (0,)))
                    if base is not None:
                        m = m + dot(q_ref[r, :], base.astype(BF16), ((1,), (0,)))
                    loc[r, at] = m
                    return
                level = n.bit_length() - 1
                add = lam[level:level + 1] * sums[(lo_c, n // 2)]
                walk(lo_c, n // 2, base)
                walk(lo_c + n // 2, n // 2, add if base is None else base + add)

            walk(0, blocks, None)

    def lam_at(level, quarter):
        return lam_ref[level:level + 1, pl.ds(pl.multiple_of(quarter * qw, qw), qw)]

    def bit(b):
        return (s >> b & 1).astype(F32)

    c0 = s_send(0, tb, rsib, s ^ 1)
    w_send(a_pos < A - 1, s, True, blk(clamp(a_pos + 1, A), b_pos, core), wa.at[0, a_pos])
    w_send(a_pos > 0, s, True, blk(clamp(a_pos - 1, A), b_pos, core), wa.at[1, a_pos])
    row = lax.broadcasted_iota(jnp.int32, (BLOCK, BLOCK), 0)
    col = lax.broadcasted_iota(jnp.int32, (BLOCK, BLOCK), 1)
    for c in range(blocks):
        r = pl.ds(c * BLOCK, BLOCK)
        scores = dot(q_ref[r, :], k_ref[r, :], ((1,), (1,)))
        gsc[c] = jnp.where(row >= col, scores, 0.0).astype(BF16)
    c0.wait()
    first = 2 * core
    for i in range(2):
        t = tot[first + i] + rsib[first + i].astype(F32)
        half_f[i] = t
        half_b[i] = t.astype(BF16)
    c1 = s_send(1, half_b, r1, s ^ 2)
    cut = [tiles * i // (nbits - 1) for i in range(nbits)]
    local_tiles(cut[0], cut[1])
    c1.wait()
    mine = s >> 1 & 1
    send_b(True, a_pos, True)
    qf[...] = half_f[mine] + r1[mine].astype(F32)
    for i in range(2):
        half_f[i] = bit(1) * lam_at(levels + 2, first + i) * r1[i].astype(F32)
    for b in range(2, nbits):
        qb[b - 2] = qf[...].astype(BF16)
        cb = s_send(b, qb.at[b - 2], rq.at[b - 2], s ^ (1 << b))
        if b == 2:
            send_core(True, a_pos, b_pos, True)
        local_tiles(cut[b - 1], cut[b])
        cb.wait()
        got = rq[b - 2].astype(F32)
        half_f[mine] += bit(b) * lam_at(levels + 1 + b, first + mine) * got
        contrib = bit(b) * lam_at(levels + 1 + b, first + mine) * got
        if b == 2:
            xs[1] = contrib
        else:
            xs[1] += contrib
        qf[...] += got
        if b == 2:
            step_a(1)
    qb[nbits - 2] = xs[1].astype(BF16)
    cx = s_send(nbits, qb.at[nbits - 2], xr, s ^ 2)
    cx.wait()
    half_f[1 - mine] += xr[...].astype(F32)
    hs[...] = half_f[...].astype(BF16)
    ch = s_send(nbits + 1, hs, hr, s ^ 1)
    for j in range(2, A):
        if j == 2:
            step_a(j)
    ch.wait()
    other = 2 - first
    for i in range(2):
        acr[first + i] = (half_f[i] + bit(0) * lam_at(levels + 1, first + i) * rsib[first + i].astype(F32)).astype(BF16)
        acr[other + i] = (
            hr[i].astype(F32) + bit(0) * lam_at(levels + 1, other + i) * rsib[other + i].astype(F32)
        ).astype(BF16)
    gate_copy.wait()

    rt = 128
    row_tiles = tok // rt

    @pl.loop(0, row_tiles)
    def _(t):
        r = pl.ds(pl.multiple_of(t * rt, rt), rt)
        squares = jnp.zeros((rt, 1), F32)
        for i in range(4):
            at = slice(i * qw, (i + 1) * qw)
            mixed = loc[r, at] + dot(q_ref[r, :], acr[i], ((1,), (0,)))
            g = gate[r, at].astype(F32)
            gated = mixed * (g / (1.0 + jnp.exp(-g)))
            squares = squares + jnp.sum(gated * gated, axis=1, keepdims=True)
            gbuf[r, at] = (gated * gain_ref[:, at]).astype(BF16)
        wide = jnp.broadcast_to(squares, (rt, 128)).T
        ssq_own[:, r] = wide[0:8]

    sq = []
    for d in range(1, H):
        copy = remote(ssq_own, ssq_all.at[d], qs.at[d], qr.at[d], {"head": (h + d) % H})
        copy.start()
        sq.append(copy)

    for j in range(3, A):
        step_a(j)
    steps_b()
    for i in range(A * B):
        w_wait(True, blk(i // B, i % B, 1 - core), wc.at[0])
    own_copy.wait()

    nj, nw = psend.shape[1], psend.shape[3]
    per = nw // mr
    pt = 256
    ptiles = tok // pt

    def product(head, j, t):
        first_block = head * (nj * per) + j * per
        w = wbuf[pl.ds(first_block, per)].reshape(nw, cols)
        r = pl.ds(pl.multiple_of(t * pt, pt), pt)
        return dot(gbuf[r, :], w, ((1,), (1,))).astype(BF16), r

    def p_copy(d, j, t):
        r = pl.ds(pl.multiple_of(t * pt, pt), pt)
        return remote(
            psend.at[d, j, r], precv.at[d, j, r], ps.at[d, j, t], pr.at[d, j, t], {"head": (h + d) % H}
        )

    for d in range(1, H):
        @pl.loop(0, nj * ptiles)
        def _(i):
            j, t = i // ptiles, i % ptiles
            val, r = product((h + d) % H, j, t)
            psend[d, j, r] = val
            p_copy(d, j, t).start()

    @pl.loop(0, nj * ptiles)
    def _(i):
        j, t = i // ptiles, i % ptiles
        val, r = product(h, j, t)
        pown[j, r] = val

    for copy in sq:
        copy.wait()

    @pl.loop(0, ptiles)
    def _(t):
        r = pl.ds(pl.multiple_of(t * pt, pt), pt)
        total = ssq_own[:, r]
        for d in range(1, H):
            total = total + ssq_all[d, :, r]
        wide = jnp.broadcast_to(total[0:1], (128, pt)).T
        loc[r, 0:128] = lax.rsqrt(wide / INNER + EPSILON)

    for j in range(nj):
        @pl.loop(0, ptiles)
        def _(t):
            r = pl.ds(pl.multiple_of(t * pt, pt), pt)
            acc = pown[j, r].astype(F32)
            for d in range(1, H):
                p_copy(d, j, t).wait_recv()
                acc = acc + precv[d, j, r].astype(F32)
            scale = loc[r, 0:128][:, 0:1]
            out_ref[r, j * nw:(j + 1) * nw] = (acc * scale).astype(BF16)

    for d in range(1, H):
        @pl.loop(0, nj * ptiles)
        def _(i):
            p_copy(d, i // ptiles, i % ptiles).wait_send()
    for cond, copy in pending:
        when(cond, lambda: copy.wait_send())


def body(query_rows, key_rows, value_rows, gate_rows, norm_gain, level_table, level_index, out_weight):
    S, H = lax.axis_size("seq"), lax.axis_size("head")
    tok, state = query_rows.shape
    cols = value_rows.shape[1]
    mr = out_weight.shape[0]
    head_width = cols // level_index.shape[0]
    nlev = level_index.shape[1]
    blocks = tok // BLOCK
    nbits = S.bit_length() - 1
    choose = (level_index[:, :, None] == jnp.arange(level_table.shape[0], dtype=jnp.int32)).astype(F32)
    picked = jnp.sum(choose * level_table, axis=2)
    tiers = jnp.arange(nlev)
    bucket_sizes = BLOCK * jnp.exp2(jnp.maximum(tiers - 1, 0).astype(F32))
    weights = picked / jnp.sqrt(bucket_sizes)
    lam = jnp.repeat(weights, head_width, axis=0).T
    model_here = mr * S // H
    nw = min(512, model_here)
    nj = model_here // nw
    qw = cols // 4
    A = min(4, S // 2)
    B = S // (2 * A)
    ptiles = tok // 256
    vm = pl.BlockSpec(memory_space=pltpu.VMEM)
    hbm = pl.BlockSpec(memory_space=pl.ANY)
    dma = pltpu.SemaphoreType.DMA
    return pl.pallas_call(
        functools.partial(kernel, S, H),
        out_shape=jax.ShapeDtypeStruct((tok, model_here), BF16),
        in_specs=[vm, vm, vm, hbm, vm, vm, hbm],
        out_specs=vm,
        scratch_shapes=[
            pltpu.VMEM((tok, cols), BF16),
            pltpu.VMEM((S, mr, cols), BF16),
            pltpu.VMEM((tok, cols), F32),
            pltpu.VMEM((tok, cols), BF16),
            pltpu.VMEM((blocks, BLOCK, BLOCK), BF16),
            pltpu.VMEM((4, state, qw), F32),
            pltpu.VMEM((4, state, qw), BF16),
            pltpu.VMEM((4, state, qw), BF16),
            pltpu.VMEM((2, state, qw), F32),
            pltpu.VMEM((2, state, qw), BF16),
            pltpu.VMEM((2, state, qw), BF16),
            pltpu.VMEM((state, qw), F32),
            pltpu.VMEM((nbits, state, qw), BF16),
            pltpu.VMEM((nbits, state, qw), BF16),
            pltpu.VMEM((2, state, qw), F32),
            pltpu.VMEM((state, qw), BF16),
            pltpu.VMEM((2, state, qw), BF16),
            pltpu.VMEM((2, state, qw), BF16),
            pltpu.VMEM((4, state, qw), BF16),
            pltpu.VMEM((8, tok), F32),
            pltpu.VMEM((H, 8, tok), F32),
            pltpu.VMEM((H, nj, tok, nw), BF16),
            pltpu.VMEM((H, nj, tok, nw), BF16),
            pltpu.VMEM((nj, tok, nw), BF16),
            dma((2,)),
            dma((nbits + 2,)),
            dma((nbits + 2,)),
            dma((S,)),
            dma((2, A)),
            dma((2, A * B)),
            dma((A * B,)),
            dma((H,)),
            dma((H,)),
            dma((H, nj, ptiles)),
            dma((H, nj, ptiles)),
        ],
        compiler_params=pltpu.CompilerParams(
            collective_id=0, has_side_effects=True, vmem_limit_bytes=66 * 2**20 - 3 * 2**20
        ),
    )(query_rows, key_rows, value_rows, gate_rows, norm_gain.reshape(1, cols), lam, out_weight)


def solution(mesh):
    in_specs = (
        P("seq", None),
        P("seq", None),
        P("seq", "head"),
        P("seq", "head"),
        P("head"),
        P(),
        P("head", None),
        P("seq", "head"),
    )
    return jax.shard_map(body, mesh=mesh, in_specs=in_specs, out_specs=P("seq", "head"), check_vma=False)
```

time: 258 us -> 136 us (0.53)
  waiting for transfers between devices: 137 us -> 0 us
  Pallas kernels: 0 us -> 130 us
  other arithmetic: 42.3 us -> 0.91 us
  matrix products: 33.9 us -> 0 us
  local copies, waits for them, and re-layouts: 19.9 us -> 4.66 us
  between operations: 13.6 us -> 0.03 us
  starting transfers between devices: 6.89 us -> 0 us
  blocking collectives: 4.91 us -> 0 us
    pallas_call x0 -> x1, Pallas kernels: none -> 130 us  [body(): pl.pallas_call(functools.partial(kernel, S, H), out_shape=jax.ShapeDtypeS...]
    ppermute x4 -> x0, waiting for transfers between devices: 82.4 us -> none  [partner_2(): return lax.ppermute(block, axis, route)]
    reduce_scatter x1 -> x0, waiting for transfers between devices: 53.4 us -> none  [body(): lax.psum_scatter(partial_rows.astype(jnp.bfloat16), 'head', scatter_dimen...]
    dot_general x4 -> x0, matrix products: 33.9 us -> none  [the longest x1 15.3 us: body(): lax.dot_general(normed, lax.all_gather(out_weight, 'seq', axis=0, tiled=T...]
    another operation x3 -> x0, local copies, waits for them, and re-layouts: 18.2 us -> none  [body(): jnp.stack([jnp.zeros_like(lower_sum), lower_sum * column_weights[tier_num...]
    reduce_sum x4 -> x0, other arithmetic: 14.5 us -> none  [the longest x1 7.67 us: body(): square_sum = lax.psum(jnp.sum(gated_rows * gated_rows, axis=1), 'head')]
    convert_element_type x2 -> x0, other arithmetic: 11.8 us -> none  [the longest x1 11.8 us: body(): carried = (combined + across[None]).astype(jnp.bfloat16)]
    ppermute x4 -> x0, starting transfers between devices: 6.85 us -> none  [partner_2(): return lax.ppermute(block, axis, route)]
  transfers between devices with their start and end apart: 6 -> 0, of which waited for: 4 -> 0; matrix products, arithmetic and copies ran while one was open for 31% -> 0% of each run, Pallas kernels for 0% -> 0%
where the time goes in v1:
time: 136 us; the launch traced here: 135 us
  Pallas kernels  130 us (96%)
  local copies, waits for them, and re-layouts  4.66 us (3%)
    pallas_call x1, Pallas kernels, body(): pl.pallas_call(functools.partial(kernel, S, H), out_shape=jax.ShapeDtypeS...  130 us
    unnamed x5, local copies, waits for them, and re-layouts  4.66 us

profile of v1, /device:TPU:0, one launch (start us, length us, event | category | flops | bytes accessed | tf_op | source)
XLA Modules:
  0.0 135.2 jit_solution(17967593903901522441)
XLA Ops:
  0.0 0.8 copy.9
  0.8 0.8 select_reduce_fusion
  1.6 0.1 broadcast_divide_fusion
  1.7 0.1 broadcast_bitcast_fusion
  1.8 0.7 copy.10
  2.5 129.6 %shard_map.82 = bf16[1024,1024]{1,0:T(8,128)(2,1)} custom-call(bf16[1024,128]{1,0:T(8,128)(2,1)} %q_ref.1, bf16[1024,128]{1,0:T(8,128)(2,1)} %k_ref.1, bf16[1024,2048]{1,0:T(8,128)(2,1)} %v_ref.1, bf16[1024,2048]{1,0:T(8,128)(2,1)} %gate_hbm.1, f32[1,2048]{1,0:T(1,128)} %bitcast.11, f32[11,2048]{1,0:T(8,128)} %bitcast.9, bf16[128,2048]{1,0:T(8,128)(2,1)} %w_hbm.1), custom_call_target="tpu_custom_call" | custom-call | tf_op jit(solution)/shard_map/pallas_call | solution.py:353
  132.1 3.1 %copy.12 = bf16[1024,1024]{1,0:T(8,128)(2,1)} copy(bf16[1024,1024]{1,0:T(8,128)(2,1)} %shard_map.82) | data formatting | bytes 4194304
  (2 shorter events, 0.0 us)

commit v2 on v1

--- a/solution.py
+++ b/solution.py
@@ -95,33 +95,46 @@
     def send_core(cond, ab, bb, own):
         w_send(cond, blk(ab, bb, core), own, s ^ 1, wc.at[ab * B + bb])
 
+    def urgent(ab):
+        return ab * H // A != h
+
+    def source_a(j, sign):
+        ab = a_pos - sign * j
+        cond = ab >= 0 if sign == 1 else ab <= A - 1
+        return cond, clamp(ab, A)
+
+    def across_b(j, first):
+        if j == 0:
+            send_b(urgent(a_pos) if first else jnp.logical_not(urgent(a_pos)), a_pos, True)
+            return
+        for sign in (1, -1):
+            cond, ab = source_a(j, sign)
+            send_b(both(cond, urgent(ab) if first else jnp.logical_not(urgent(ab))), ab, False)
+
     def step_a(j):
         for sign in (1, -1):
-            ab = a_pos - sign * j
-            cond = ab >= 0 if sign == 1 else ab <= A - 1
-            ab = clamp(ab, A)
+            cond, ab = source_a(j, sign)
             block = blk(ab, b_pos, core)
             w_wait(cond, block, wc.at[0])
             onward = a_pos < A - 1 if sign == 1 else a_pos > 0
             nxt = clamp(a_pos + sign, A)
             w_send(both(cond, onward), block, False, blk(nxt, b_pos, core), wa.at[(1 - sign) // 2, ab])
-            send_b(cond, ab, False)
             send_core(cond, ab, b_pos, False)
 
-    def steps_b():
+    def finish(ab):
         for j in range(1, B):
             for sign in (1, -1):
                 bb = b_pos - sign * j
                 cond = bb >= 0 if sign == 1 else bb <= B - 1
                 bb = clamp(bb, B)
                 onward = both(cond, b_pos < B - 1 if sign == 1 else b_pos > 0)
-                for i in range(A):
-                    ab = lax.rem(a_pos + i, A)
-                    block = blk(ab, bb, core)
-                    w_wait(cond, block, wc.at[0])
-                    if B > 2:
-                        w_send(onward, block, False, blk(a_pos, clamp(b_pos + sign, B), core), wb.at[(1 - sign) // 2, ab * B + bb])
-                    send_core(cond, ab, bb, False)
+                block = blk(ab, bb, core)
+                w_wait(cond, block, wc.at[0])
+                if B > 2:
+                    w_send(onward, block, False, blk(a_pos, clamp(b_pos + sign, B), core), wb.at[(1 - sign) // 2, ab * B + bb])
+                send_core(cond, ab, bb, False)
+        for bb in range(B):
+            w_wait(True, blk(ab, bb, 1 - core), wc.at[0])
 
     def s_send(i, src, dst, target):
         copy = remote(src, dst, ssem.at[i], rsem.at[i], {"seq": target})
@@ -190,20 +203,21 @@
         half_f[i] = t
         half_b[i] = t.astype(BF16)
     c1 = s_send(1, half_b, r1, s ^ 2)
+    across_b(0, True)
+    send_core(True, a_pos, b_pos, True)
     cut = [tiles * i // (nbits - 1) for i in range(nbits)]
     local_tiles(cut[0], cut[1])
     c1.wait()
     mine = s >> 1 & 1
-    send_b(True, a_pos, True)
     qf[...] = half_f[mine] + r1[mine].astype(F32)
     for i in range(2):
         half_f[i] = bit(1) * lam_at(levels + 2, first + i) * r1[i].astype(F32)
     for b in range(2, nbits):
         qb[b - 2] = qf[...].astype(BF16)
         cb = s_send(b, qb.at[b - 2], rq.at[b - 2], s ^ (1 << b))
-        if b == 2:
-            send_core(True, a_pos, b_pos, True)
         local_tiles(cut[b - 1], cut[b])
+        if b == nbits - 1:
+            step_a(1)
         cb.wait()
         got = rq[b - 2].astype(F32)
         half_f[mine] += bit(b) * lam_at(levels + 1 + b, first + mine) * got
@@ -213,17 +227,13 @@
         else:
             xs[1] += contrib
         qf[...] += got
-        if b == 2:
-            step_a(1)
     qb[nbits - 2] = xs[1].astype(BF16)
     cx = s_send(nbits, qb.at[nbits - 2], xr, s ^ 2)
+    across_b(1, True)
     cx.wait()
     half_f[1 - mine] += xr[...].astype(F32)
     hs[...] = half_f[...].astype(BF16)
     ch = s_send(nbits + 1, hs, hr, s ^ 1)
-    for j in range(2, A):
-        if j == 2:
-            step_a(j)
     ch.wait()
     other = 2 - first
     for i in range(2):
@@ -232,6 +242,9 @@
             hr[i].astype(F32) + bit(0) * lam_at(levels + 1, other + i) * rsib[other + i].astype(F32)
         ).astype(BF16)
     gate_copy.wait()
+    for j in range(2, min(3, A)):
+        step_a(j)
+        across_b(j, True)
 
     rt = 128
     row_tiles = tok // rt
@@ -256,11 +269,6 @@
         copy.start()
         sq.append(copy)
 
-    for j in range(3, A):
-        step_a(j)
-    steps_b()
-    for i in range(A * B):
-        w_wait(True, blk(i // B, i % B, 1 - core), wc.at[0])
     own_copy.wait()
 
     nj, nw = psend.shape[1], psend.shape[3]
@@ -280,19 +288,49 @@
             psend.at[d, j, r], precv.at[d, j, r], ps.at[d, j, t], pr.at[d, j, t], {"head": (h + d) % H}
         )
 
-    for d in range(1, H):
-        @pl.loop(0, nj * ptiles)
-        def _(i):
-            j, t = i // ptiles, i % ptiles
+    def far_steps():
+        for j in range(3, A):
+            step_a(j)
+            across_b(j, True)
+        for j in range(A):
+            across_b(j, False)
+
+    def send_chunk(d, j):
+        @pl.loop(0, ptiles)
+        def _(t):
             val, r = product((h + d) % H, j, t)
             psend[d, j, r] = val
             p_copy(d, j, t).start()
 
-    @pl.loop(0, nj * ptiles)
-    def _(i):
-        j, t = i // ptiles, i % ptiles
-        val, r = product(h, j, t)
-        pown[j, r] = val
+    def own_chunk(j):
+        @pl.loop(0, ptiles)
+        def _(t):
+            val, r = product(h, j, t)
+            pown[j, r] = val
+
+    one_row = H == 2 and nj * H == A
+    order = list(range(nj))
+    if one_row:
+        low = (1 - h) * nj
+        near = jnp.where(jnp.abs(low - a_pos) <= jnp.abs(low + 1 - a_pos), 0, 1)
+        order = [near, 1 - near]
+        for i, j in enumerate(order):
+            if i == 1:
+                far_steps()
+            finish(low + j)
+            send_chunk(1, j)
+        for j in range(nj):
+            finish(h * nj + j)
+            own_chunk(j)
+    else:
+        far_steps()
+        for i in range(A):
+            finish(i)
+        for d in range(1, H):
+            for j in range(nj):
+                send_chunk(d, j)
+        for j in range(nj):
+            own_chunk(j)
 
     for copy in sq:
         copy.wait()
@@ -308,7 +346,7 @@
 
     for j in range(nj):
         @pl.loop(0, ptiles)
-        def _(t):
+        def _(t, j=j):
             r = pl.ds(pl.multiple_of(t * pt, pt), pt)
             acc = pown[j, r].astype(F32)
             for d in range(1, H):

time: 136 us -> 109 us (0.80)
  Pallas kernels: 130 us -> 102 us
    pallas_call x1, Pallas kernels: 130 us -> 102 us  [body(): pl.pallas_call(functools.partial(kernel, S, H), out_shape=jax.ShapeDtypeS...]
where the time goes in v2:
time: 109 us; the launch traced here: 108 us
  Pallas kernels  102 us (94%)
  local copies, waits for them, and re-layouts  4.66 us (4%)
    pallas_call x1, Pallas kernels, body(): pl.pallas_call(functools.partial(kernel, S, H), out_shape=jax.ShapeDtypeS...  102 us
    unnamed x5, local copies, waits for them, and re-layouts  4.66 us

profile of v2, /device:TPU:0, one launch (start us, length us, event | category | flops | bytes accessed | tf_op | source)
XLA Modules:
  0.0 107.6 jit_solution(17121354709536799602)
XLA Ops:
  0.0 0.8 copy.9
  0.8 0.8 select_reduce_fusion
  1.6 0.1 broadcast_divide_fusion
  1.7 0.1 broadcast_bitcast_fusion
  1.8 0.7 copy.10
  2.5 102.0 %shard_map.82 = bf16[1024,1024]{1,0:T(8,128)(2,1)} custom-call(bf16[1024,128]{1,0:T(8,128)(2,1)} %q_ref.1, bf16[1024,128]{1,0:T(8,128)(2,1)} %k_ref.1, bf16[1024,2048]{1,0:T(8,128)(2,1)} %v_ref.1, bf16[1024,2048]{1,0:T(8,128)(2,1)} %gate_hbm.1, f32[1,2048]{1,0:T(1,128)} %bitcast.11, f32[11,2048]{1,0:T(8,128)} %bitcast.9, bf16[128,2048]{1,0:T(8,128)(2,1)} %w_hbm.1), custom_call_target="tpu_custom_call" | custom-call | tf_op jit(solution)/shard_map/pallas_call | solution.py:391
  104.5 3.1 %copy.12 = bf16[1024,1024]{1,0:T(8,128)(2,1)} copy(bf16[1024,1024]{1,0:T(8,128)(2,1)} %shard_map.82) | data formatting | bytes 4194304
  (2 shorter events, 0.0 us)

commit v3 on v2

--- a/solution.py
+++ b/solution.py
@@ -105,7 +105,7 @@
 
     def across_b(j, first):
         if j == 0:
-            send_b(urgent(a_pos) if first else jnp.logical_not(urgent(a_pos)), a_pos, True)
+            send_b(True, a_pos, True)
             return
         for sign in (1, -1):
             cond, ab = source_a(j, sign)
@@ -121,7 +121,10 @@
             w_send(both(cond, onward), block, False, blk(nxt, b_pos, core), wa.at[(1 - sign) // 2, ab])
             send_core(cond, ab, b_pos, False)
 
-    def finish(ab):
+    def finish_own(ab):
+        w_wait(True, blk(ab, b_pos, 1 - core), wc.at[0])
+
+    def finish_rest(ab):
         for j in range(1, B):
             for sign in (1, -1):
                 bb = b_pos - sign * j
@@ -133,8 +136,8 @@
                 if B > 2:
                     w_send(onward, block, False, blk(a_pos, clamp(b_pos + sign, B), core), wb.at[(1 - sign) // 2, ab * B + bb])
                 send_core(cond, ab, bb, False)
-        for bb in range(B):
-            w_wait(True, blk(ab, bb, 1 - core), wc.at[0])
+        for j in range(1, B):
+            w_wait(True, blk(ab, lax.rem(b_pos + j, B), 1 - core), wc.at[0])
 
     def s_send(i, src, dst, target):
         copy = remote(src, dst, ssem.at[i], rsem.at[i], {"seq": target})
@@ -292,7 +295,7 @@
         for j in range(3, A):
             step_a(j)
             across_b(j, True)
-        for j in range(A):
+        for j in range(1, A):
             across_b(j, False)
 
     def send_chunk(d, j):
@@ -308,24 +311,32 @@
             val, r = product(h, j, t)
             pown[j, r] = val
 
-    one_row = H == 2 and nj * H == A
-    order = list(range(nj))
-    if one_row:
-        low = (1 - h) * nj
+    paired = H == 2 and A == 4 and B == 2 and nj == 4
+
+    def chunk_order(half):
+        low = half * 2
         near = jnp.where(jnp.abs(low - a_pos) <= jnp.abs(low + 1 - a_pos), 0, 1)
-        order = [near, 1 - near]
+        return [2 * near + b_pos, 2 * near + 1 - b_pos, 2 * (1 - near) + b_pos, 2 * (1 - near) + 1 - b_pos]
+
+    arrivals = list(range(nj))
+    if paired:
+        order = chunk_order(1 - h)
+        arrivals = chunk_order(h)
         for i, j in enumerate(order):
-            if i == 1:
+            if i == 2:
                 far_steps()
-            finish(low + j)
+            ab = (1 - h) * 2 + j // 2
+            finish_own(ab) if i % 2 == 0 else finish_rest(ab)
             send_chunk(1, j)
-        for j in range(nj):
-            finish(h * nj + j)
+        for i, j in enumerate(arrivals):
+            ab = h * 2 + j // 2
+            finish_own(ab) if i % 2 == 0 else finish_rest(ab)
             own_chunk(j)
     else:
         far_steps()
         for i in range(A):
-            finish(i)
+            finish_own(i)
+            finish_rest(i)
         for d in range(1, H):
             for j in range(nj):
                 send_chunk(d, j)
@@ -344,7 +355,7 @@
         wide = jnp.broadcast_to(total[0:1], (128, pt)).T
         loc[r, 0:128] = lax.rsqrt(wide / INNER + EPSILON)
 
-    for j in range(nj):
+    for j in arrivals:
         @pl.loop(0, ptiles)
         def _(t, j=j):
             r = pl.ds(pl.multiple_of(t * pt, pt), pt)
@@ -353,7 +364,7 @@
                 p_copy(d, j, t).wait_recv()
                 acc = acc + precv[d, j, r].astype(F32)
             scale = loc[r, 0:128][:, 0:1]
-            out_ref[r, j * nw:(j + 1) * nw] = (acc * scale).astype(BF16)
+            out_ref[r, pl.ds(pl.multiple_of(j * nw, nw), nw)] = (acc * scale).astype(BF16)
 
     for d in range(1, H):
         @pl.loop(0, nj * ptiles)
@@ -379,7 +390,7 @@
     weights = picked / jnp.sqrt(bucket_sizes)
     lam = jnp.repeat(weights, head_width, axis=0).T
     model_here = mr * S // H
-    nw = min(512, model_here)
+    nw = min(256, model_here)
     nj = model_here // nw
     qw = cols // 4
     A = min(4, S // 2)

time: 109 us -> 103 us (0.945)
  Pallas kernels: 102 us -> 96.9 us
    pallas_call x1, Pallas kernels: 102 us -> 96.9 us  [body(): pl.pallas_call(functools.partial(kernel, S, H), out_shape=jax.ShapeDtypeS...]
where the time goes in v3:
time: 103 us
  Pallas kernels  96.9 us (94%)
  local copies, waits for them, and re-layouts  4.66 us (5%)
    pallas_call x1, Pallas kernels, body(): pl.pallas_call(functools.partial(kernel, S, H), out_shape=jax.ShapeDtypeS...  96.9 us
    unnamed x5, local copies, waits for them, and re-layouts  4.66 us

profile of v3, /device:TPU:0, one launch (start us, length us, event | category | flops | bytes accessed | tf_op | source)
XLA Modules:
  0.0 102.6 jit_solution(18321043354655363911)
XLA Ops:
  0.0 0.8 copy.9
  0.8 0.8 select_reduce_fusion
  1.6 0.1 broadcast_divide_fusion
  1.7 0.1 broadcast_bitcast_fusion
  1.8 0.7 copy.10
  2.5 96.9 %shard_map.82 = bf16[1024,1024]{1,0:T(8,128)(2,1)} custom-call(bf16[1024,128]{1,0:T(8,128)(2,1)} %q_ref.1, bf16[1024,128]{1,0:T(8,128)(2,1)} %k_ref.1, bf16[1024,2048]{1,0:T(8,128)(2,1)} %v_ref.1, bf16[1024,2048]{1,0:T(8,128)(2,1)} %gate_hbm.1, f32[1,2048]{1,0:T(1,128)} %bitcast.11, f32[11,2048]{1,0:T(8,128)} %bitcast.9, bf16[128,2048]{1,0:T(8,128)(2,1)} %w_hbm.1), custom_call_target="tpu_custom_call" | custom-call | tf_op jit(solution)/shard_map/pallas_call | solution.py:402
  99.5 3.1 %copy.12 = bf16[1024,1024]{1,0:T(8,128)(2,1)} copy(bf16[1024,1024]{1,0:T(8,128)(2,1)} %shard_map.82) | data formatting | bytes 4194304
  (2 shorter events, 0.0 us)

commit v4 on v3

--- a/solution.py
+++ b/solution.py
@@ -323,7 +323,7 @@
         order = chunk_order(1 - h)
         arrivals = chunk_order(h)
         for i, j in enumerate(order):
-            if i == 2:
+            if i == 1:
                 far_steps()
             ab = (1 - h) * 2 + j // 2
             finish_own(ab) if i % 2 == 0 else finish_rest(ab)

time: 103 us -> 103 us (level)
  no operation moved by 1% of the time
where the time goes in v4:
time: 103 us
  Pallas kernels  96.9 us (94%)
  local copies, waits for them, and re-layouts  4.66 us (5%)
    pallas_call x1, Pallas kernels, body(): pl.pallas_call(functools.partial(kernel, S, H), out_shape=jax.ShapeDtypeS...  96.9 us
    unnamed x5, local copies, waits for them, and re-layouts  4.66 us

profile of v4, /device:TPU:0, one launch (start us, length us, event | category | flops | bytes accessed | tf_op | source)
XLA Modules:
  0.0 102.6 jit_solution(10871816326227167926)
XLA Ops:
  0.0 0.8 copy.9
  0.8 0.8 select_reduce_fusion
  1.6 0.1 broadcast_divide_fusion
  1.7 0.1 broadcast_bitcast_fusion
  1.8 0.7 copy.10
  2.5 96.9 %shard_map.82 = bf16[1024,1024]{1,0:T(8,128)(2,1)} custom-call(bf16[1024,128]{1,0:T(8,128)(2,1)} %q_ref.1, bf16[1024,128]{1,0:T(8,128)(2,1)} %k_ref.1, bf16[1024,2048]{1,0:T(8,128)(2,1)} %v_ref.1, bf16[1024,2048]{1,0:T(8,128)(2,1)} %gate_hbm.1, f32[1,2048]{1,0:T(1,128)} %bitcast.11, f32[11,2048]{1,0:T(8,128)} %bitcast.9, bf16[128,2048]{1,0:T(8,128)(2,1)} %w_hbm.1), custom_call_target="tpu_custom_call" | custom-call | tf_op jit(solution)/shard_map/pallas_call | solution.py:402
  99.5 3.1 %copy.12 = bf16[1024,1024]{1,0:T(8,128)(2,1)} copy(bf16[1024,1024]{1,0:T(8,128)(2,1)} %shard_map.82) | data formatting | bytes 4194304
  (2 shorter events, 0.0 us)
